TPU v7x, 256 devices: a whole 4x4x8 slice. The times are simulated.
256 devices in a mesh: dp: 64 (over z, x, core), rep: 4 (over y).
Axes of the slice: x: 4, y: 4, z: 8, core: 2. Of those that a mesh axis runs over, the one named last changes fastest.
Arguments:
- ecg: bfloat16 [4, 327680], P('rep', 'dp'), may hold values from -6 to 6
- conv_first: bfloat16 [5, 256], replicated, may hold values from -2.5 to 2.5
- conv_second: bfloat16 [512, 256], replicated, may hold values from -0.25 to 0.25
- conv_third: bfloat16 [512, 256], replicated, may hold values from -0.25 to 0.25
- enc_gain: float32 [256], replicated, may hold values from 0.1 to 1.9
- ctx_weight: bfloat16 [2, 512, 256], replicated, may hold values from -0.25 to 0.25
- head_weight: bfloat16 [256, 12, 256], replicated, may hold values from -0.375 to 0.375
- sources: int32 [4, 512, 4, 2], P('rep', 'dp'), may hold values from 0 to 63, as said below
Outputs:
- target_grad: float32 [4, 16384, 256], P('rep', 'dp')
- head_grad: float32 [4, 256, 12, 256], P('rep')
Inputs may be any that keep to these rules, and one draw needn't show every extreme that they name: sources[r, i, s] = (o, b): o is the piece index along the recording, b a block of 128 rows of that piece's 256 positions. Among the 32 entries of one piece at most 2 name the same piece o, and in every draw one piece o is named exactly 2 times by every piece of its recording.
All inputs are finite; a program needn't handle non-finite values.
Results may differ from a plain program's by a relative error of at most 0.0085.
Values may be sent and summed in bfloat16 or wider, within the bound.
No kernel may reach another device: no remote copies, remote signals or barrier semaphores. Data moves between devices by JAX's collectives and lax.ppermute only.
A program may use at most 128 MiB of HBM per device.

v0:
```python
import math

import jax
import jax.numpy as jnp
from jax import lax
from jax.sharding import PartitionSpec as P


def gelu_exact(values):
    return jax.nn.gelu(values, approximate=False)


def encode(piece, conv_first, conv_second, conv_third, enc_gain, ctx_weight):
    channels = conv_first.shape[1]
    positions = piece.shape[0] // 20
    frames = piece.reshape(4 * positions, 5)
    hidden_one = gelu_exact(jnp.dot(frames, conv_first, preferred_element_type=jnp.float32)).astype(
        jnp.bfloat16
    )
    hidden_two = gelu_exact(
        jnp.dot(
            hidden_one.reshape(2 * positions, 2 * channels),
            conv_second,
            preferred_element_type=jnp.float32,
        )
    ).astype(jnp.bfloat16)
    mixed = jnp.dot(
        hidden_two.reshape(positions, 2 * channels), conv_third, preferred_element_type=jnp.float32
    )
    average = jnp.mean(mixed, -1, keepdims=True)
    centred = mixed - average
    variance = jnp.mean(centred * centred, -1, keepdims=True)
    latent = (centred / jnp.sqrt(variance + 1e-05) * enc_gain).astype(jnp.bfloat16)
    latent_wide = latent.astype(jnp.float32)
    target = (
        latent_wide / jnp.sqrt(jnp.sum(latent_wide * latent_wide, -1, keepdims=True) + 1e-06)
    ).astype(jnp.bfloat16)
    context = latent
    for layer_index in range(ctx_weight.shape[0]):
        dilation = 2**layer_index
        before = jnp.concatenate(
            [jnp.zeros((dilation, channels), jnp.bfloat16), context[: positions - dilation]], 0
        )
        joined = jnp.concatenate([context, before], 1)
        update = gelu_exact(
            jnp.dot(joined, ctx_weight[layer_index], preferred_element_type=jnp.float32)
        )
        context = (context.astype(jnp.float32) + update).astype(jnp.bfloat16)
    return (target, context)


def score_piece(target, context, head_weight, negatives):
    positions, channels = target.shape
    horizon = head_weight.shape[1]
    groups = negatives.shape[0]
    pred = jnp.dot(
        context,
        head_weight.reshape(channels, horizon * channels),
        preferred_element_type=jnp.float32,
    ).reshape(positions, horizon, channels)
    pred_norm = jnp.sqrt(jnp.sum(pred * pred, -1, keepdims=True) + 1e-06)
    unit_pred = pred / pred_norm
    queries = unit_pred.astype(jnp.bfloat16)
    shifted = jnp.stack(
        [
            jnp.concatenate(
                [target[step_index + 1 :], jnp.zeros((step_index + 1, channels), jnp.bfloat16)], 0
            )
            for step_index in range(horizon)
        ],
        1,
    )
    usable = (
        lax.broadcasted_iota(jnp.int32, (positions, horizon), 0)
        + lax.broadcasted_iota(jnp.int32, (positions, horizon), 1)
        + 1
        < positions
    ).astype(jnp.float32)
    positive = 10.0 * jnp.sum(queries.astype(jnp.float32) * shifted.astype(jnp.float32), -1)
    grouped = queries.reshape(groups, -1, channels)
    negative = 10.0 * jnp.einsum(
        "gqc,gnc->gqn", grouped, negatives, preferred_element_type=jnp.float32
    )
    pos_exp = jnp.exp(positive)
    neg_exp = jnp.exp(negative)
    partition = pos_exp.reshape(groups, -1) + jnp.sum(neg_exp, -1)
    usable_grouped = usable.reshape(groups, -1)
    pos_weight = 10.0 * usable * (pos_exp / partition.reshape(positions, horizon) - 1.0)
    neg_weight = (10.0 * usable_grouped[:, :, None] * neg_exp / partition[:, :, None]).astype(
        jnp.bfloat16
    )
    neg_part = jnp.einsum("gqn,gnc->gqc", neg_weight, negatives, preferred_element_type=jnp.float32)
    query_grad = pos_weight[:, :, None] * shifted.astype(jnp.float32) + neg_part.reshape(
        positions, horizon, channels
    )
    neg_grad = jnp.einsum(
        "gqn,gqc->gnc", neg_weight, grouped, preferred_element_type=jnp.float32
    ).astype(jnp.bfloat16)
    pos_terms = pos_weight[:, :, None] * queries.astype(jnp.float32)
    pos_grad = jnp.zeros((positions, channels), jnp.float32)
    for step_index in range(horizon):
        moved = jnp.concatenate(
            [
                jnp.zeros((step_index + 1, channels), jnp.float32),
                pos_terms[: positions - step_index - 1, step_index],
            ],
            0,
        )
        pos_grad = pos_grad + moved
    radial = jnp.sum(unit_pred * query_grad, -1, keepdims=True)
    pred_grad = (
        ((query_grad - unit_pred * radial) / pred_norm)
        .astype(jnp.bfloat16)
        .reshape(positions, horizon * channels)
    )
    head_part = lax.dot_general(
        context, pred_grad, (((0,), (0,)), ((), ())), preferred_element_type=jnp.float32
    )
    return (pos_grad, neg_grad, head_part)


def local(ecg, conv_first, conv_second, conv_third, enc_gain, ctx_weight, head_weight, sources):
    owner_total = lax.axis_size("dp")
    groups = sources.shape[1]
    entries = sources.reshape(-1, 2)
    owner_id = entries[:, 0]
    block_id = entries[:, 1]
    entry_count = entries.shape[0]
    capacity = max(2, 2 * entry_count // owner_total)
    slot_total = owner_total * capacity
    earlier = lax.broadcasted_iota(jnp.int32, (entry_count, entry_count), 1) < lax.broadcasted_iota(
        jnp.int32, (entry_count, entry_count), 0
    )
    same_owner = owner_id[:, None] == owner_id[None, :]
    rank_of = jnp.sum((earlier & same_owner).astype(jnp.int32), 1)
    slot_of = owner_id * capacity + rank_of
    matches = slot_of[:, None] == jnp.arange(slot_total, dtype=jnp.int32)[None, :]
    wanted = jnp.sum(jnp.where(matches, block_id[:, None], 0), 0).reshape(owner_total, capacity)
    occupied = jnp.any(matches, 0)
    entry_of = jnp.sum(jnp.where(matches, jnp.arange(entry_count, dtype=jnp.int32)[:, None], 0), 0)
    requested = lax.all_to_all(wanted, "dp", split_axis=0, concat_axis=0, tiled=True)
    target, context = encode(
        ecg.reshape(-1), conv_first, conv_second, conv_third, enc_gain, ctx_weight
    )
    positions, channels = target.shape
    segment = lax.all_gather(target, "dp", axis=0, tiled=True)
    piece_count = segment.shape[0] // positions
    segment_blocks = segment.reshape(piece_count, positions // 128, 128, channels)
    chosen = jnp.take_along_axis(segment_blocks, wanted[:, :, None, None], axis=1)
    chosen = chosen.reshape(piece_count * capacity, 128, channels)
    fetched = jnp.take(chosen, slot_of, axis=0)
    negatives = fetched.reshape(groups, -1, channels)
    pos_grad, neg_grad, head_part = score_piece(target, context, head_weight, negatives)
    horizon = head_weight.shape[1]
    neg_blocks = neg_grad.reshape(entry_count, 128, channels)
    picked = jnp.take(neg_blocks, entry_of, axis=0)
    outgoing = jnp.where(occupied[:, None, None], picked, jnp.zeros_like(picked)).reshape(
        owner_total, capacity, 128, channels
    )
    returned = lax.all_to_all(outgoing, "dp", split_axis=0, concat_axis=0, tiled=True).reshape(
        slot_total, 128 * channels
    )
    placed = (
        requested.reshape(-1)[None, :] == jnp.arange(positions // 128, dtype=jnp.int32)[:, None]
    ).astype(jnp.bfloat16)
    summed = jnp.dot(placed, returned, preferred_element_type=jnp.float32).reshape(
        positions, channels
    )
    target_grad = ((pos_grad + summed) / horizon)[None]
    head_total = lax.psum(head_part, "dp")
    factor = math.sqrt(channels / (lax.axis_size("dp") * positions))
    head_grad = (head_total * factor).reshape(1, channels, horizon, channels)
    return (target_grad, head_grad)


def solution(mesh):
    in_specs = (P("rep", "dp"), P(), P(), P(), P(), P(), P(), P("rep", "dp", None, None))
    out_specs = (P("rep", "dp", None), P("rep", None, None, None))
    return jax.shard_map(local, mesh=mesh, in_specs=in_specs, out_specs=out_specs, check_vma=False)
```

profile of v0, /device:TPU:1, one launch (start us, length us, event | category | flops | bytes accessed | tf_op | source)
XLA Modules:
  0.0 484.7 jit_solution(15221614664519750533)
XLA Ops:
  8.5 3.0 fusion.12
  16.0 13.5 %all-to-all-start = ((s32[64,1,2]{2,1,0:T(1,128)}), s32[64,1,2]{2,1,0:T(1,128)}, u32[]{:S(2)}, u32[]{:S(2)}) async-start(s32[64,1,2]{2,1,0:T(1,128)} %bitcast.38), calls=%async_computation | async-start | bytes 65536 | tf_op jit(solution)/shard_map/all_to_all | solution.py:141
  29.7 1.6 slice.139
  32.8 1.6 slice.137
  38.5 1.6 slice.133
  40.1 1.6 slice.132
  44.9 1.6 slice.129
  59.9 1.9 fusion.32
  66.3 2.3 copy.45
  68.6 2.5 reshape.248
  71.3 30.8 %all-gather.2.cloned.1.call-done = bf16[16384,256]{1,0:T(8,128)(2,1)} async-done(((bf16[256,256]{1,0:T(8,128)(2,1)}), bf16[16384,256]{1,0:T(8,128)(2,1)}) %all-gather.2.cloned.1.call-update) | async-done | bytes 8388624 | tf_op jit(solution)/shard_map/all_gather | solution.py:146
  102.1 10.6 %gather_fusion.2 = bf16[128,128,256]{2,1,0:T(8,128)(2,1)} fusion(bf16[64,2,128,256]{3,2,1,0:T(8,128)(2,1)} %bitcast.130, s32[128]{0:T(128)S(1)} %reshape.273), kind=kCustom, calls=%fused_computation.2 | custom fusion | bytes 16778240 | tf_op jit(solution)/shard_map/jit(take_along_axis)/gather | solution.py:149
  112.7 7.4 %broadcast_select_fusion = bf16[128,128,256]{2,1,0:T(8,128)(2,1)} fusion(bf16[128,128,256]{2,1,0:T(8,128)(2,1)} %gather_fusion.2, pred[128]{0:T(512)(128)(4,1)S(1)} %compare_and_fusion.1), kind=kLoop, calls=%fused_computation.5 | loop fusion | flops 4194304 | bytes 16777344 | tf_op jit(solution)/shard_map/jit(take_along_axis)/select_n | solution.py:149
  120.1 5.4 %gather_fusion = bf16[32,128,256]{2,1,0:T(8,128)(2,1)} fusion(bf16[128,128,256]{2,1,0:T(8,128)(2,1)} %broadcast_select_fusion, s32[1024]{0:T(1024)S(1)} %get-tuple-element.29), kind=kCustom, calls=%fused_computation | custom fusion | bytes 4194432 | tf_op jit(solution)/shard_map/jit(_take)/gather | solution.py:151
  125.5 1.9 bitcast_select_fusion
  127.5 3.8 fusion.1
  131.8 3.8 divide_convert_fusion
  137.3 6.4 %gather_fusion.1 = bf16[128,128,256]{2,1,0:T(8,128)(2,1)} fusion(bf16[32,128,256]{2,1,0:T(8,128)(2,1)S(1)} %bitcast.125, s32[1024]{0:T(1024)S(1)} %get-tuple-element.28), kind=kCustom, calls=%fused_computation.1 | custom fusion | bytes 16777728 | tf_op jit(solution)/shard_map/jit(_take)/gather | solution.py:156
  143.7 7.4 %select_select_fusion = bf16[64,2,128,256]{3,2,1,0:T(8,128)(2,1)} fusion(bf16[64,2,128,256]{3,2,1,0:T(8,128)(2,1)} %bitcast.126, pred[64,2]{1,0:T(8,128)(4,1)S(1)} %compare_and_fusion, pred[64,2]{1,0:T(8,128)(4,1)S(1)} %copy-done.27), kind=kLoop, calls=%fused_computation.4 | loop fusion | flops 8388608 | bytes 16777472 | tf_op jit(solution)/shard_map/jit(_where)/select_n | solution.py:157
  151.1 6.6 %all-to-all-start.1 = ((bf16[64,2,128,256]{3,2,1,0:T(8,128)(2,1)}), bf16[64,2,128,256]{3,2,1,0:T(8,128)(2,1)}, u32[]{:S(2)}, u32[]{:S(2)}) async-start(bf16[64,2,128,256]{3,2,1,0:T(8,128)(2,1)} %select_select_fusion), calls=%async_computation.1 | async-start | bytes 16777216 | tf_op jit(solution)/shard_map/all_to_all | solution.py:160
  159.9 4.2 fusion.105
  164.1 4.8 reshape.254
  168.9 21.8 %divide_convert_fusion.1 = bf16[256,12,256]{2,0,1:T(8,128)(2,1)} fusion(f32[256,12]{0,1:T(8,128)S(1)} %add_sqrt_fusion, f32[256,12,256]{2,1,0:T(8,128)} %reshape.254, bf16[256,12,256]{2,0,1:T(8,128)(2,1)} %copy-done.12, f32[256,12]{0,1:T(8,128)S(1)} %get-tuple-element.18, f32[256,12,256]{2,0,1:T(8,128)S(1)} %copy-done.11), kind=kOutput, calls=%fused_computation.14 | output fusion | flops 10226943 | bytes 9461760 | tf_op jit(solution)/shard_map/mul | solution.py:112
  190.8 1.7 copy.53
  192.5 2.3 fusion.106
  203.9 245.6 %all-reduce.28.cloned.1.call-done = f32[256,3072]{1,0:T(8,128)} async-done(((f32[256,3072]{1,0:T(8,128)}), f32[256,3072]{1,0:T(8,128)}) %all-reduce.28.cloned.1.call-update) | async-done | bytes 3145744 | tf_op jit(solution)/shard_map/psum | solution.py:170
  449.6 2.1 broadcast_multiply_fusion
  451.7 2.3 copy.54
  454.0 3.8 copy.55
  457.8 12.3 %copy.58 = bf16[16,8,128,256]{3,1,2,0:T(8,128)(2,1)} copy(bf16[16,8,128,256]{3,2,1,0:T(8,128)(2,1)} %bitcast.52) | data formatting | bytes 16777216
  470.3 4.7 fusion.90
  475.3 2.1 multiply_bitcast_fusion
  (169 shorter events, 46.2 us)
Async XLA Ops:
  7.2 4.5 copy-start
  7.2 94.9 %all-gather.2.cloned.1.call-start = ((), (), s32[]{:S(2)}) async-start(), calls=%async_computation.2 | async-start | bytes 8519680 | tf_op jit(solution)/shard_map/all_gather | solution.py:146
  13.1 36.9 %copy-start.13 = (bf16[256,12,256]{2,0,1:T(8,128)(2,1)S(1)}, bf16[256,12,256]{2,0,1:T(8,128)(2,1)}, u32[]{:S(2)}) copy-start(bf16[256,12,256]{2,0,1:T(8,128)(2,1)} %param.14) | copy-start | bytes 4718596
  14.7 31.8 %copy-start.4 = (bf16[256,256]{1,0:T(8,128)(2,1)S(1)}, bf16[256,256]{1,0:T(8,128)(2,1)}, u32[]{:S(2)}) copy-start(bf16[256,256]{1,0:T(8,128)(2,1)} %fusion.34) | copy-start | bytes 393220
  15.1 34.6 %copy-start.33 = (s32[32,1]{0,1:T(1,128)}, s32[32,1]{0,1:T(1,128)S(1)}, u32[]{:S(2)}) copy-start(s32[32,1]{0,1:T(1,128)S(1)} %get-tuple-element.15) | copy-start | bytes 388
  15.2 20.8 %copy-start.28 = (s32[128]{0:T(128)}, s32[128]{0:T(128)S(1)}, u32[]{:S(2)}) copy-start(s32[128]{0:T(128)S(1)} %get-tuple-element.11) | copy-start | bytes 1540
  15.2 34.5 %copy-start.31 = (s32[128]{0:T(128)}, s32[128]{0:T(128)S(1)}, u32[]{:S(2)}) copy-start(s32[128]{0:T(128)S(1)} %get-tuple-element.10) | copy-start | bytes 1540
  16.0 135.1 %all-to-all-start = ((s32[64,1,2]{2,1,0:T(1,128)}), s32[64,1,2]{2,1,0:T(1,128)}, u32[]{:S(2)}, u32[]{:S(2)}) async-start(s32[64,1,2]{2,1,0:T(1,128)} %bitcast.38), calls=%async_computation | async-start | bytes 65536 | tf_op jit(solution)/shard_map/all_to_all | solution.py:141
  49.7 10.1 %copy-start.24 = (bf16[244,256]{1,0:T(8,128)(2,1)S(1)}, bf16[244,256]{1,0:T(8,128)(2,1)}, u32[]{:S(2)}) copy-start(bf16[244,256]{1,0:T(8,128)(2,1)} %slice.139) | copy-start | bytes 374788
  66.3 4.8 copy-start.34
  66.3 4.8 copy-start.32
  66.3 4.8 copy-start.29
  66.3 4.9 %copy-start.36 = (pred[8,4]{0,1:T(4,128)(4,1)S(1)}, pred[8,4]{0,1:T(4,128)(4,1)}, u32[]{:S(2)}) copy-start(pred[8,4]{0,1:T(4,128)(4,1)} %copy.47) | copy-start | bytes 100
  66.3 5.0 %copy-start.26 = (s32[64,2]{1,0:T(8,128)S(1)}, s32[64,2]{1,0:T(8,128)}, u32[]{:S(2)}) copy-start(s32[64,2]{1,0:T(8,128)} %reduce_sum.109) | copy-start | bytes 1540
  71.1 56.4 %copy-start.8 = (bf16[8,384,256]{2,1,0:T(8,128)(2,1)}, bf16[8,384,256]{2,1,0:T(8,128)(2,1)S(1)}, u32[]{:S(2)}) copy-start(bf16[8,384,256]{2,1,0:T(8,128)(2,1)S(1)} %reshape.248) | copy-start | bytes 4718596
  131.7 3.9 copy-start.9
  137.3 6.4 %copy-start.27 = (pred[64,2]{1,0:T(8,128)(4,1)S(1)}, pred[64,2]{1,0:T(8,128)(4,1)}, u32[]{:S(2)}) copy-start(pred[64,2]{1,0:T(8,128)(4,1)} %broadcast_in_dim.116) | copy-start | bytes 388
  151.1 8.8 %copy-start.3 = (bf16[8,384,512]{2,1,0:T(8,128)(2,1)S(1)}, bf16[8,384,512]{2,1,0:T(8,128)(2,1)}, u32[]{:S(2)}) copy-start(bf16[8,384,512]{2,1,0:T(8,128)(2,1)} %copy-done.2) | copy-start | bytes 9437188
  151.1 306.7 %all-to-all-start.1 = ((bf16[64,2,128,256]{3,2,1,0:T(8,128)(2,1)}), bf16[64,2,128,256]{3,2,1,0:T(8,128)(2,1)}, u32[]{:S(2)}, u32[]{:S(2)}) async-start(bf16[64,2,128,256]{3,2,1,0:T(8,128)(2,1)} %select_select_fusion), calls=%async_computation.1 | async-start | bytes 16777216 | tf_op jit(solution)/shard_map/all_to_all | solution.py:160
  157.7 291.9 %all-reduce.28.cloned.1.call-start = ((), (), s32[]{:S(2)}) async-start(), calls=%async_computation.3 | async-start | bytes 6291456 | tf_op jit(solution)/shard_map/psum | solution.py:170
  164.1 4.8 copy-start.11
  470.2 5.0 %copy-start.14 = (f32[249,256]{1,0:T(8,128)S(1)}, f32[249,256]{1,0:T(8,128)}, u32[]{:S(2)}) copy-start(f32[249,256]{1,0:T(8,128)} %slice_bitcast_fusion) | copy-start | bytes 764932
  470.2 5.1 %copy-start.15 = (f32[250,256]{1,0:T(8,128)S(1)}, f32[250,256]{1,0:T(8,128)}, u32[]{:S(2)}) copy-start(f32[250,256]{1,0:T(8,128)} %slice_bitcast_fusion.1) | copy-start | bytes 768004
  470.2 5.1 %copy-start.16 = (f32[251,256]{1,0:T(8,128)S(1)}, f32[251,256]{1,0:T(8,128)}, u32[]{:S(2)}) copy-start(f32[251,256]{1,0:T(8,128)} %slice_bitcast_fusion.2) | copy-start | bytes 771076
  470.2 5.1 %copy-start.17 = (f32[252,256]{1,0:T(8,128)S(1)}, f32[252,256]{1,0:T(8,128)}, u32[]{:S(2)}) copy-start(f32[252,256]{1,0:T(8,128)} %slice_bitcast_fusion.3) | copy-start | bytes 774148
  470.2 5.1 %copy-start.18 = (f32[253,256]{1,0:T(8,128)S(1)}, f32[253,256]{1,0:T(8,128)}, u32[]{:S(2)}) copy-start(f32[253,256]{1,0:T(8,128)} %slice_bitcast_fusion.4) | copy-start | bytes 777220
  470.2 5.1 %copy-start.19 = (f32[254,256]{1,0:T(8,128)S(1)}, f32[254,256]{1,0:T(8,128)}, u32[]{:S(2)}) copy-start(f32[254,256]{1,0:T(8,128)} %slice_bitcast_fusion.5) | copy-start | bytes 780292
  470.2 5.1 %copy-start.20 = (f32[255,256]{1,0:T(8,128)S(1)}, f32[255,256]{1,0:T(8,128)}, u32[]{:S(2)}) copy-start(f32[255,256]{1,0:T(8,128)} %slice_bitcast_fusion.6) | copy-start | bytes 783364
  470.2 5.1 %copy-start.21 = (f32[244,256]{1,0:T(8,128)S(1)}, f32[244,256]{1,0:T(8,128)}, u32[]{:S(2)}) copy-start(f32[244,256]{1,0:T(8,128)} %slice_bitcast_fusion.7) | copy-start | bytes 749572
  470.2 5.1 %copy-start.22 = (f32[245,256]{1,0:T(8,128)S(1)}, f32[245,256]{1,0:T(8,128)}, u32[]{:S(2)}) copy-start(f32[245,256]{1,0:T(8,128)} %slice_bitcast_fusion.8) | copy-start | bytes 752644
  470.2 5.1 %copy-start.23 = (f32[246,256]{1,0:T(8,128)S(1)}, f32[246,256]{1,0:T(8,128)}, u32[]{:S(2)}) copy-start(f32[246,256]{1,0:T(8,128)} %slice_bitcast_fusion.9) | copy-start | bytes 755716
  470.2 7.2 %copy-start.1 = (bf16[512,256]{1,0:T(8,128)(2,1)S(1)}, bf16[512,256]{1,0:T(8,128)(2,1)}, u32[]{:S(2)}) copy-start(bf16[512,256]{1,0:T(8,128)(2,1)} %param.10) | copy-start | bytes 786436
  (10 other events, 22.6 us)
Sparse Core Ops, SparseCore 0:
  14.9 87.1 all-gather.1
  194.9 254.6 all-reduce.27
where the time goes:
time: 491 us; the launch traced here: 485 us
  waiting for transfers between devices  277 us (56%)
  local copies, waits for them, and re-layouts  95.9 us (20%)
  other arithmetic  52.4 us (11%)
  matrix products  24.5 us (5%)
  starting transfers between devices  20.2 us (4%)
  between operations  15.3 us (3%)
    psum x1, waiting for transfers between devices, local(): head_total = lax.psum(head_part, 'dp')  246 us
    all_gather x1, waiting for transfers between devices, local(): segment = lax.all_gather(target, 'dp', axis=0, tiled=True)  30.8 us
    unnamed x91, local copies, waits for them, and re-layouts  28.1 us
    mul x1, other arithmetic, score_piece(): unit_pred * radial  21.8 us
    slice x12, local copies, waits for them, and re-layouts, score_piece(): target[step_index + 1:]  17.5 us
    all_to_all x1, starting transfers between devices, local(): lax.all_to_all(wanted, 'dp', split_axis=0, concat_axis=0, tiled=True)  13.5 us
    gather x2, local copies, waits for them, and re-layouts, local(): jnp.take_along_axis(segment_blocks, wanted[:, :, None, None], axis=1)  10.7 us
  transfers between devices with their start and end apart: 4, of which 2 were waited for; matrix products, arithmetic and copies ran while one was open for 30% of the time, Pallas kernels for 0%

commit v1 on v0

v1 whole, which is shorter than its diff:
```python
import math

import jax
import jax.numpy as jnp
from jax import lax
from jax.experimental import pallas as pl
from jax.experimental.pallas import tpu as pltpu
from jax.sharding import Mesh, PartitionSpec as P

BF = jnp.bfloat16
F32 = jnp.float32
Z_ORDER = (4, 3, -3, 2, -2, 1, -1, 0)
Z_BUNDLES = (3, 4, 1)


def gelu_exact(values):
    return jax.nn.gelu(values, approximate=False)


def encode(piece, conv_first, conv_second, conv_third, enc_gain, ctx_weight):
    channels = conv_first.shape[1]
    positions = piece.shape[0] // 20
    frames = piece.reshape(4 * positions, 5)
    hidden_one = gelu_exact(jnp.dot(frames, conv_first, preferred_element_type=F32)).astype(BF)
    hidden_two = gelu_exact(
        jnp.dot(
            hidden_one.reshape(2 * positions, 2 * channels),
            conv_second,
            preferred_element_type=F32,
        )
    ).astype(BF)
    mixed = jnp.dot(
        hidden_two.reshape(positions, 2 * channels), conv_third, preferred_element_type=F32
    )
    average = jnp.mean(mixed, -1, keepdims=True)
    centred = mixed - average
    variance = jnp.mean(centred * centred, -1, keepdims=True)
    latent = (centred / jnp.sqrt(variance + 1e-05) * enc_gain).astype(BF)
    latent_wide = latent.astype(F32)
    target = (
        latent_wide / jnp.sqrt(jnp.sum(latent_wide * latent_wide, -1, keepdims=True) + 1e-06)
    ).astype(BF)
    context = latent
    for layer_index in range(ctx_weight.shape[0]):
        dilation = 2**layer_index
        before = jnp.concatenate(
            [jnp.zeros((dilation, channels), BF), context[: positions - dilation]], 0
        )
        joined = jnp.concatenate([context, before], 1)
        update = gelu_exact(jnp.dot(joined, ctx_weight[layer_index], preferred_element_type=F32))
        context = (context.astype(F32) + update).astype(BF)
    return (target, context)


def score_kernel(
    where_ref, tgt_ref, ctx_ref, hw_ref, *rest, horizon, groups, per_group, positions, bank_count
):
    banks = rest[:bank_count]
    keep_ref, send_ref, hkeep_ref, hsend_ref, pos_ref = rest[bank_count : bank_count + 5]
    nbuf, q_s, t_s, pg_s, p_s, inv_s, sc_s, pad_s, sems = rest[bank_count + 5 :]
    rows = positions // groups
    entries = groups * per_group

    def start(e, carry):
        bank_id = where_ref[0, e]
        row = where_ref[1, e]
        for a in range(bank_count):

            @pl.when(bank_id == a)
            def _():
                pltpu.make_async_copy(banks[a].at[row], nbuf.at[e], sems.at[e]).start()

        return carry

    lax.fori_loop(0, entries, start, 0)

    keep_ref[...] = jnp.zeros(keep_ref.shape, BF)
    send_ref[...] = jnp.zeros(send_ref.shape, BF)

    pad_s[:positions] = tgt_ref[...].astype(F32)
    pad_s[positions:] = jnp.zeros((16, pad_s.shape[1]), F32)
    for k in range(horizon):
        pred = jnp.dot(ctx_ref[...], hw_ref[k], preferred_element_type=F32)
        inv = 1.0 / jnp.sqrt(jnp.sum(pred * pred, -1, keepdims=True) + 1e-06)
        query = (pred * inv).astype(BF)
        shifted = pad_s[k + 1 : k + 1 + positions]
        score = 10.0 * jnp.sum(query.astype(F32) * shifted, -1, keepdims=True)
        part = slice(k * rows, (k + 1) * rows)
        q_s[:, part, :] = query.reshape(groups, rows, -1)
        t_s[:, part, :] = shifted.astype(BF).reshape(groups, rows, -1)
        inv_s[:, part, :] = inv.reshape(groups, rows, 1)
        sc_s[:, part, :] = score.reshape(groups, rows, 1)

    row_id = lax.broadcasted_iota(jnp.int32, (horizon * rows, 1), 0)
    step_id = row_id // rows
    local_id = row_id - step_id * rows

    def group(g, carry):
        for s in range(per_group):
            e = g * per_group + s
            pltpu.make_async_copy(banks[0].at[0], nbuf.at[e], sems.at[e]).wait()
        queries = q_s[g]
        negatives = nbuf[pl.ds(g * per_group, per_group)].reshape(per_group * 128, -1)
        negative = lax.dot_general(
            queries, negatives, (((1,), (1,)), ((), ())), preferred_element_type=F32
        )
        neg_exp = jnp.exp(10.0 * negative)
        pos_exp = jnp.exp(sc_s[g])
        partition = pos_exp + jnp.sum(neg_exp, -1, keepdims=True)
        usable = ((g * rows + local_id + step_id + 1) < positions).astype(F32)
        over = 10.0 * usable / partition
        weight = (neg_exp * over).astype(BF)
        pos_weight = pos_exp * over - 10.0 * usable
        neg_part = jnp.dot(weight, negatives, preferred_element_type=F32)
        neg_grad = lax.dot_general(
            weight, queries, (((0,), (0,)), ((), ())), preferred_element_type=F32
        )
        for s in range(per_group):
            e = g * per_group + s
            place = where_ref[2, e]
            block = neg_grad[s * 128 : (s + 1) * 128]

            @pl.when(where_ref[3, e] == 0)
            def _():
                keep_ref[place] = (keep_ref[place].astype(F32) + block).astype(BF)

            @pl.when(where_ref[3, e] != 0)
            def _():
                send_ref[place] = (send_ref[place].astype(F32) + block).astype(BF)

        unit = queries.astype(F32)
        query_grad = pos_weight * t_s[g].astype(F32) + neg_part
        radial = jnp.sum(unit * query_grad, -1, keepdims=True)
        pred_grad = ((query_grad - unit * radial) * inv_s[g]).astype(BF)
        pos_term = pos_weight * unit
        at = pl.ds(pl.multiple_of(g * rows, rows), rows)
        for k in range(horizon):
            pg_s[k, at, :] = pred_grad[k * rows : (k + 1) * rows]
            p_s[k, at, :] = pos_term[k * rows : (k + 1) * rows]
        return carry

    lax.fori_loop(0, groups, group, 0)

    core = where_ref[4, 0]
    half = horizon // 2

    def head(i, carry):
        for ref, base in ((hkeep_ref, core), (hsend_ref, 1 - core)):
            part = lax.dot_general(
                ctx_ref[...],
                pg_s[base * half + i],
                (((0,), (0,)), ((), ())),
                preferred_element_type=F32,
            )
            ref[i] = part.astype(BF)
        return carry

    lax.fori_loop(0, half, head, 0)
    pad_s[...] = jnp.zeros(pad_s.shape, F32)
    for k in range(horizon):
        at = slice(k + 1, k + 1 + positions)
        pad_s[at] = pad_s[at] + p_s[k]
    pos_ref[...] = pad_s[:positions]


def score(where, target, context, head_maps, banks, groups, per_group):
    positions, channels = target.shape
    horizon = head_maps.shape[0]
    blocks = 2 * (positions // 128) * banks[0].shape[0]
    rows = horizon * positions // groups
    vmem = pl.BlockSpec(memory_space=pltpu.VMEM)
    hbm = pl.BlockSpec(memory_space=pl.ANY)
    return pl.pallas_call(
        lambda *refs: score_kernel(
            *refs,
            horizon=horizon,
            groups=groups,
            per_group=per_group,
            positions=positions,
            bank_count=len(banks),
        ),
        out_shape=(
            jax.ShapeDtypeStruct((blocks, 128, channels), BF),
            jax.ShapeDtypeStruct((blocks, 128, channels), BF),
            jax.ShapeDtypeStruct((horizon // 2, channels, channels), BF),
            jax.ShapeDtypeStruct((horizon // 2, channels, channels), BF),
            jax.ShapeDtypeStruct((positions, channels), F32),
        ),
        in_specs=[pl.BlockSpec(memory_space=pltpu.SMEM), vmem, vmem, vmem] + [hbm] * len(banks),
        out_specs=(vmem,) * 5,
        scratch_shapes=[
            pltpu.VMEM((groups * per_group, 128, channels), BF),
            pltpu.VMEM((groups, rows, channels), BF),
            pltpu.VMEM((groups, rows, channels), BF),
            pltpu.VMEM((horizon, positions, channels), BF),
            pltpu.VMEM((horizon, positions, channels), F32),
            pltpu.VMEM((groups, rows, 1), F32),
            pltpu.VMEM((groups, rows, 1), F32),
            pltpu.VMEM((positions + 16, channels), F32),
            pltpu.SemaphoreType.DMA((groups * per_group,)),
        ],
        name="score",
    )(where, target, context, head_maps, *banks)


def shift(values, axis, by):
    size = lax.axis_size(axis)
    return lax.ppermute(values, axis, [(i, (i + by) % size) for i in range(size)])


def exchange(values, axis):
    return lax.all_to_all(values, axis, 0, 0, tiled=True)


def add(*terms):
    total = terms[0].astype(F32)
    for term in terms[1:]:
        total = total + term.astype(F32)
    return total


def gather_targets(target):
    z_size = lax.axis_size("z")
    row = exchange(jnp.broadcast_to(target[None], (z_size,) + target.shape), "z")
    left = shift(row, "x", 1)
    right = shift(row, "x", -1)
    far_low = shift(left[:, :128], "x", 1)
    far_high = shift(right[:, 128:], "x", -1)
    mine = [row, left, right, far_low, far_high]
    return mine + [shift(v, "c", 1) for v in mine]


def reduce_x(here, ahead, behind, far):
    low = shift(far[:, :128], "x", 1)
    high = shift(far[:, 128:], "x", -1)
    ahead = jnp.concatenate([add(ahead[:, :128], low).astype(BF), ahead[:, 128:]], 1)
    behind = jnp.concatenate([behind[:, :128], add(behind[:, 128:], high).astype(BF)], 1)
    return add(here, shift(ahead, "x", 1), shift(behind, "x", -1))


def return_blocks(keep, send):
    received = shift(send, "c", 1)
    total = None
    first = 0
    for count in Z_BUNDLES:
        parts = [
            add(keep[d, first : first + count], received[d, first : first + count]).astype(BF)
            for d in (0, 1, 3, 2)
        ]
        sums = reduce_x(*parts)
        for i in range(count):
            by = Z_ORDER[first + i]
            term = sums[i] if by == 0 else shift(sums[i].astype(BF), "z", by).astype(F32)
            total = term if total is None else total + term
        first += count
    return total


def reduce_heads(keep, send):
    x_size, z_size = lax.axis_size("x"), lax.axis_size("z")
    channels = keep.shape[-1]
    part = add(keep, shift(send, "c", 1)).astype(BF).reshape(x_size, z_size, -1, channels)
    part = jnp.sum(exchange(part, "x").astype(F32), 0).astype(BF)
    part = jnp.sum(exchange(part, "z").astype(F32), 0).astype(BF)
    part = exchange(jnp.broadcast_to(part[None], (z_size,) + part.shape), "z")
    part = exchange(jnp.broadcast_to(part[None], (x_size,) + part.shape), "x")
    part = part.reshape(keep.shape)
    other = shift(part, "c", 1)
    core = lax.axis_index("c")
    return jnp.concatenate(
        [jnp.where(core == 0, part, other), jnp.where(core == 0, other, part)], 0
    )


def local(ecg, conv_first, conv_second, conv_third, enc_gain, ctx_weight, head_weight, sources):
    z_size, x_size, c_size = (lax.axis_size(a) for a in ("z", "x", "c"))
    groups, per_group = sources.shape[1:3]
    z_id, x_id, c_id = (lax.axis_index(a) for a in ("z", "x", "c"))
    owner = sources[0, :, :, 0].reshape(-1)
    block = sources[0, :, :, 1].reshape(-1)
    owner_z = owner // (x_size * c_size)
    owner_x = (owner // c_size) % x_size
    other_core = (owner % c_size != c_id).astype(jnp.int32)
    dx = (owner_x - x_id) % x_size
    dz = (owner_z - z_id) % z_size
    bank = jnp.where(
        dx == 0, 0, jnp.where(dx == 3, 1, jnp.where(dx == 1, 2, 3 + block))
    ) + 5 * other_core
    bank_row = jnp.where(dx == 2, owner_z, 2 * owner_z + block)
    position = jnp.where(dz == 0, 7, jnp.where(dz == 4, 0, jnp.where(dz < 4, 7 - 2 * dz, 2 * dz - 8)))
    place = 2 * (dx * z_size + position) + block
    where = jnp.stack(
        [bank, bank_row, place, other_core, jnp.full_like(bank, 0) + c_id]
    ).astype(jnp.int32)

    target, context = encode(
        ecg.reshape(-1), conv_first, conv_second, conv_third, enc_gain, ctx_weight
    )
    positions, channels = target.shape
    horizon = head_weight.shape[1]
    banks = [v.reshape(-1, 128, channels) for v in gather_targets(target)]
    keep, send, head_keep, head_send, pos_grad = score(
        where, target, context, head_weight.transpose(1, 0, 2), banks, groups, per_group
    )
    shape = (x_size, z_size, positions, channels)
    summed = return_blocks(keep.reshape(shape), send.reshape(shape))
    target_grad = ((pos_grad + summed) / horizon)[None]
    heads = reduce_heads(head_keep, head_send)
    factor = math.sqrt(channels / (z_size * x_size * c_size * positions))
    head_grad = (heads.astype(F32) * factor).transpose(1, 0, 2)[None]
    return (target_grad, head_grad)


def solution(mesh):
    fine = Mesh(mesh.devices.reshape(8, 4, 2, -1), ("z", "x", "c", "rep"))
    dp = ("z", "x", "c")
    in_specs = (P("rep", dp), P(), P(), P(), P(), P(), P(), P("rep", dp, None, None))
    out_specs = (P("rep", dp, None), P("rep", None, None, None))
    return jax.shard_map(local, mesh=fine, in_specs=in_specs, out_specs=out_specs, check_vma=False)
```

time: 491 us -> 259 us (0.53)
  waiting for transfers between devices: 277 us -> 57.4 us
  local copies, waits for them, and re-layouts: 95.9 us -> 5.96 us
  blocking collectives: 0 us -> 84.7 us
  other arithmetic: 52.4 us -> 16.1 us
  starting transfers between devices: 20.2 us -> 56.4 us
  Pallas kernels: 0 us -> 23.5 us
  matrix products: 24.5 us -> 7.9 us
  between operations: 15.3 us -> 1.38 us
    psum x1 -> x0, waiting for transfers between devices: 246 us -> none  [local(): head_total = lax.psum(head_part, 'dp')]
    all_to_all x0 -> x5, blocking collectives: none -> 84.7 us  [exchange(): return lax.all_to_all(values, axis, 0, 0, tiled=True)]
    ppermute x0 -> x31, waiting for transfers between devices: none -> 57.4 us  [shift(): lax.ppermute(values, axis, [(i, (i + by) % size) for i in range(size)])]
    ppermute x0 -> x31, starting transfers between devices: none -> 56.4 us  [shift(): lax.ppermute(values, axis, [(i, (i + by) % size) for i in range(size)])]
    all_gather x1 -> x0, waiting for transfers between devices: 30.8 us -> none  [local(): segment = lax.all_gather(target, 'dp', axis=0, tiled=True)]
    unnamed x91 -> x28, local copies, waits for them, and re-layouts: 28.1 us -> 1.41 us
    mul x5 -> x0, other arithmetic: 24.5 us -> none  [the longest x1 21.8 us: score_piece(): unit_pred * radial]
    pallas_call x0 -> x1, Pallas kernels: none -> 23.5 us  [score(): pl.pallas_call(lambda *refs: score_kernel(*refs, horizon=horizon, groups=...]
  transfers between devices with their start and end apart: 4 -> 31, of which waited for: 2 -> 8; matrix products, arithmetic and copies ran while one was open for 30% -> 7% of each run, Pallas kernels for 0% -> 0%
where the time goes in v1:
time: 259 us; the launch traced here: 253 us
  blocking collectives  84.7 us (33%)
  waiting for transfers between devices  57.4 us (22%)
  starting transfers between devices  56.4 us (22%)
  Pallas kernels  23.5 us (9%)
  other arithmetic  16.1 us (6%)
  matrix products  7.9 us (3%)
  local copies, waits for them, and re-layouts  5.96 us (2%)
    all_to_all x5, blocking collectives, exchange(): return lax.all_to_all(values, axis, 0, 0, tiled=True)  84.7 us
    ppermute x31, waiting for transfers between devices, shift(): lax.ppermute(values, axis, [(i, (i + by) % size) for i in range(size)])  57.4 us
    ppermute x31, starting transfers between devices, shift(): lax.ppermute(values, axis, [(i, (i + by) % size) for i in range(size)])  56.4 us
    pallas_call x1, Pallas kernels, score(): pl.pallas_call(lambda *refs: score_kernel(*refs, horizon=horizon, groups=...  23.5 us
  transfers between devices with their start and end apart: 31, of which 8 were waited for; matrix products, arithmetic and copies ran while one was open for 7% of the time, Pallas kernels for 0%

profile of v1, /device:TPU:1, one launch (start us, length us, event | category | flops | bytes accessed | tf_op | source)
XLA Modules:
  0.0 253.4 jit_solution(6682898791253514344)
XLA Ops:
  1.9 3.0 %fusion.2 = bf16[1024,256]{1,0:T(8,128)(2,1)S(1)} fusion(bf16[1024,5]{1,0:T(8,128)(2,1)S(1)} %reshape_reshape.3, bf16[5,256]{1,0:T(8,128)(2,1)} %param.9), kind=kOutput, calls=%fused_computation.5 | convolution fusion | flops 19660800 | bytes 537088 | tf_op jit(solution)/shard_map/dot_general | solution.py:24
  8.1 36.1 %all_to_all.25 = bf16[8,256,256]{2,1,0:T(8,128)(2,1)S(1)} all-to-all(bf16[8,256,256]{2,1,0:T(8,128)(2,1)S(1)} %broadcast_in_dim.16), channel_id=1, replica_groups=mesh['z'=8,'x'=4,'c'=2,'rep'=4] {'z'}, dimensions={0} | all-to-all | bytes 2097152 | tf_op jit(solution)/shard_map/all_to_all | solution.py:212
  44.2 2.4 collective-permute-start.1
  47.0 19.6 %collective-permute-done.1 = bf16[8,256,256]{2,1,0:T(8,128)(2,1)S(1)} collective-permute-done((bf16[8,256,256]{2,1,0:T(8,128)(2,1)S(1)}, bf16[8,256,256]{2,1,0:T(8,128)(2,1)S(1)}, u32[]{:S(2)}, u32[]{:S(2)}) %collective-permute-start.1) | collective-permute-done | bytes 1048608 | tf_op jit(solution)/shard_map/ppermute | solution.py:208
  67.5 3.4 %collective-permute-start.3 = (bf16[8,128,256]{2,1,0:T(8,128)(2,1)}, bf16[8,128,256]{2,1,0:T(8,128)(2,1)}, u32[]{:S(2)}, u32[]{:S(2)}) collective-permute-start(bf16[8,128,256]{2,1,0:T(8,128)(2,1)} %slice.238), channel_id=1, source_target_pairs={{0,24},{8,0},{16,8},{24,16},{1,25},{9,1},{17,9},{25,17},{2,26},{10... | collective-permute-start | bytes 1572872 | tf_op jit(solution)/shard_map/ppermute | solution.py:208
  72.4 3.7 %collective-permute-start.4 = (bf16[8,256,256]{2,1,0:T(8,128)(2,1)S(1)}, bf16[8,256,256]{2,1,0:T(8,128)(2,1)}, u32[]{:S(2)}, u32[]{:S(2)}) collective-permute-start(bf16[8,256,256]{2,1,0:T(8,128)(2,1)S(1)} %all_to_all.25), channel_id=1, source_target_pairs={{0,4},{4,0},{1,5},{5,1},{2,6},{6,2},{3,7},{7,3},{8,12},{12,8},{9,1... | collective-permute-start | bytes 3145736 | tf_op jit(solution)/shard_map/ppermute | solution.py:208
  79.1 4.3 %collective-permute-start.8 = (bf16[8,128,256]{2,1,0:T(8,128)(2,1)}, bf16[8,128,256]{2,1,0:T(8,128)(2,1)S(1)}, u32[]{:S(2)}, u32[]{:S(2)}) collective-permute-start(bf16[8,128,256]{2,1,0:T(8,128)(2,1)} %collective-permute-done.3.refs_8_), channel_id=1, source_target_pairs={{0,4},{4,0},{1,5},{5,1},{2,6},{6,2},{3,7},{7,3},{8,12},{12,8},{9,1... | collective-permute-start | bytes 1572872 | tf_op jit(solution)/shard_map/ppermute | solution.py:208
  83.4 4.5 %collective-permute-start.7 = (bf16[8,128,256]{2,1,0:T(8,128)(2,1)}, bf16[8,128,256]{2,1,0:T(8,128)(2,1)S(1)}, u32[]{:S(2)}, u32[]{:S(2)}) collective-permute-start(bf16[8,128,256]{2,1,0:T(8,128)(2,1)} %collective-permute-done.2.refs_7_), channel_id=1, source_target_pairs={{0,4},{4,0},{1,5},{5,1},{2,6},{6,2},{3,7},{7,3},{8,12},{12,8},{9,1... | collective-permute-start | bytes 1572872 | tf_op jit(solution)/shard_map/ppermute | solution.py:208
  87.9 1.9 fusion.36
  92.2 23.5 %score.1 = (bf16[64,128,256]{2,1,0:T(8,128)(2,1)}, bf16[64,128,256]{2,1,0:T(8,128)(2,1)}, bf16[6,256,256]{2,1,0:T(8,128)(2,1)}, bf16[6,256,256]{2,1,0:T(8,128)(2,1)}, f32[256,256]{1,0:T(8,128)}) custom-call(s32[5,32]{1,0:T(8,128)} %stack.2.refs_0_, bf16[256,256]{1,0:T(8,128)(2,1)} %copy-done.5, bf16[256,256]{1,0:T(8,128)(2,1)} %fusion.42.refs_2_, ...), custom_call_target="tpu_custom_call" | custom-call | tf_op jit(solution)/shard_map/score/pallas_call | solution.py:173
  116.3 7.6 %collective-permute-done.29 = bf16[6,256,256]{2,1,0:T(8,128)(2,1)S(1)} collective-permute-done((bf16[6,256,256]{2,1,0:T(8,128)(2,1)}, bf16[6,256,256]{2,1,0:T(8,128)(2,1)S(1)}, u32[]{:S(2)}, u32[]{:S(2)}) %collective-permute-start.29) | collective-permute-done | bytes 786464 | tf_op jit(solution)/shard_map/ppermute | solution.py:208
  125.2 14.4 %all_to_all.26 = bf16[4,8,48,256]{3,2,1,0:T(8,128)(2,1)S(1)} all-to-all(bf16[4,8,48,256]{3,2,1,0:T(8,128)(2,1)S(1)} %bitcast.107), channel_id=1, replica_groups=mesh['z'=8,'x'=4,'c'=2,'rep'=4] {'x'}, dimensions={0} | all-to-all | bytes 1572864 | tf_op jit(solution)/shard_map/all_to_all | solution.py:212
  139.8 12.2 %all_to_all.27 = bf16[8,48,256]{2,1,0:T(8,128)(2,1)S(1)} all-to-all(bf16[8,48,256]{2,1,0:T(8,128)(2,1)S(1)} %reduce_sum.54), channel_id=1, replica_groups=mesh['z'=8,'x'=4,'c'=2,'rep'=4] {'z'}, dimensions={0} | all-to-all | bytes 393216 | tf_op jit(solution)/shard_map/all_to_all | solution.py:212
  152.1 11.1 %all_to_all.28 = bf16[8,48,256]{2,1,0:T(8,128)(2,1)S(1)} all-to-all(bf16[8,48,256]{2,1,0:T(8,128)(2,1)S(1)} %broadcast_in_dim.18), channel_id=1, replica_groups=mesh['z'=8,'x'=4,'c'=2,'rep'=4] {'z'}, dimensions={0} | all-to-all | bytes 393216 | tf_op jit(solution)/shard_map/all_to_all | solution.py:212
  163.3 10.7 %all_to_all.29 = bf16[4,8,48,256]{3,2,1,0:T(8,128)(2,1)S(1)} all-to-all(bf16[4,8,48,256]{3,2,1,0:T(8,128)(2,1)S(1)} %broadcast_in_dim.19), channel_id=1, replica_groups=mesh['z'=8,'x'=4,'c'=2,'rep'=4] {'x'}, dimensions={0} | all-to-all | bytes 1572864 | tf_op jit(solution)/shard_map/all_to_all | solution.py:212
  174.0 5.2 %collective-permute-start.30 = (bf16[6,256,256]{2,1,0:T(8,128)(2,1)S(1)}, bf16[6,256,256]{2,1,0:T(8,128)(2,1)S(1)}, u32[]{:S(2)}, u32[]{:S(2)}) collective-permute-start(bf16[6,256,256]{2,1,0:T(8,128)(2,1)S(1)} %bitcast.108), channel_id=1, source_target_pairs={{0,4},{4,0},{1,5},{5,1},{2,6},{6,2},{3,7},{7,3},{8,12},{12,8},{9,1... | collective-permute-start | bytes 2359304 | tf_op jit(solution)/shard_map/ppermute | solution.py:208
  179.2 1.9 collective-permute-done.30
  182.9 2.4 collective-permute-start.27
  185.3 1.6 fusion.31
  187.1 12.0 %collective-permute-start.12 = (bf16[3,128,256]{2,1,0:T(8,128)(2,1)S(1)}, bf16[3,128,256]{2,1,0:T(8,128)(2,1)S(1)}, u32[]{:S(2)}, u32[]{:S(2)}) collective-permute-start(bf16[3,128,256]{2,1,0:T(8,128)(2,1)S(1)} %get-tuple-element.38), channel_id=1, source_target_pairs={{0,24},{8,0},{16,8},{24,16},{1,25},{9,1},{17,9},{25,17},{2,26},{10... | collective-permute-start | bytes 589832 | tf_op jit(solution)/shard_map/ppermute | solution.py:208
  199.1 1.8 fusion.18
  201.1 2.7 %collective-permute-start.19 = (bf16[4,128,256]{2,1,0:T(8,128)(2,1)S(1)}, bf16[4,128,256]{2,1,0:T(8,128)(2,1)S(1)}, u32[]{:S(2)}, u32[]{:S(2)}) collective-permute-start(bf16[4,128,256]{2,1,0:T(8,128)(2,1)S(1)} %get-tuple-element.33), channel_id=1, source_target_pairs={{0,24},{8,0},{16,8},{24,16},{1,25},{9,1},{17,9},{25,17},{2,26},{10... | collective-permute-start | bytes 786440 | tf_op jit(solution)/shard_map/ppermute | solution.py:208
  205.8 1.8 collective-permute-done.19
  207.7 3.5 %collective-permute-start.20 = (bf16[4,256,256]{2,1,0:T(8,128)(2,1)S(1)}, bf16[4,256,256]{2,1,0:T(8,128)(2,1)S(1)}, u32[]{:S(2)}, u32[]{:S(2)}) collective-permute-start(bf16[4,256,256]{2,1,0:T(8,128)(2,1)S(1)} %pad_maximum_fusion.1), channel_id=1, source_target_pairs={{0,24},{8,0},{16,8},{24,16},{1,25},{9,1},{17,9},{25,17},{2,26},{10... | collective-permute-start | bytes 1572872 | tf_op jit(solution)/shard_map/ppermute | solution.py:208
  211.4 7.4 %collective-permute-done.13 = bf16[3,256,256]{2,1,0:T(8,128)(2,1)S(1)} collective-permute-done((bf16[3,256,256]{2,1,0:T(8,128)(2,1)S(1)}, bf16[3,256,256]{2,1,0:T(8,128)(2,1)S(1)}, u32[]{:S(2)}, u32[]{:S(2)}) %collective-permute-start.13) | collective-permute-done | bytes 393248 | tf_op jit(solution)/shard_map/ppermute | solution.py:208
  220.5 9.5 %collective-permute-done.20 = bf16[4,256,256]{2,1,0:T(8,128)(2,1)S(1)} collective-permute-done((bf16[4,256,256]{2,1,0:T(8,128)(2,1)S(1)}, bf16[4,256,256]{2,1,0:T(8,128)(2,1)S(1)}, u32[]{:S(2)}, u32[]{:S(2)}) %collective-permute-start.20) | collective-permute-done | bytes 524320 | tf_op jit(solution)/shard_map/ppermute | solution.py:208
  230.1 3.3 %collective-permute-start.15 = (bf16[256,256]{1,0:T(8,128)(2,1)S(1)}, bf16[256,256]{1,0:T(8,128)(2,1)S(1)}, u32[]{:S(2)}, u32[]{:S(2)}) collective-permute-start(bf16[256,256]{1,0:T(8,128)(2,1)S(1)} %get-tuple-element.36), channel_id=1, source_target_pairs={{0,96},{32,128},{64,160},{96,192},{128,224},{160,0},{192,32},{224,... | collective-permute-start | bytes 393224 | tf_op jit(solution)/shard_map/ppermute | solution.py:208
  236.0 2.7 %collective-permute-start.24 = (bf16[256,256]{1,0:T(8,128)(2,1)S(1)}, bf16[256,256]{1,0:T(8,128)(2,1)S(1)}, u32[]{:S(2)}, u32[]{:S(2)}) collective-permute-start(bf16[256,256]{1,0:T(8,128)(2,1)S(1)} %get-tuple-element.29), channel_id=1, source_target_pairs={{0,224},{32,0},{64,32},{96,64},{128,96},{160,128},{192,160},{224,1... | collective-permute-start | bytes 393224 | tf_op jit(solution)/shard_map/ppermute | solution.py:208
  240.0 2.0 multiply_bitcast_fusion
  241.9 6.0 %collective-permute-done.21 = bf16[256,256]{1,0:T(8,128)(2,1)S(1)} collective-permute-done((bf16[256,256]{1,0:T(8,128)(2,1)S(1)}, bf16[256,256]{1,0:T(8,128)(2,1)S(1)}, u32[]{:S(2)}, u32[]{:S(2)}) %collective-permute-start.21) | collective-permute-done | bytes 131104 | tf_op jit(solution)/shard_map/ppermute | solution.py:208
  247.9 3.5 %collective-permute-done.23 = bf16[256,256]{1,0:T(8,128)(2,1)S(1)} collective-permute-done((bf16[256,256]{1,0:T(8,128)(2,1)S(1)}, bf16[256,256]{1,0:T(8,128)(2,1)S(1)}, u32[]{:S(2)}, u32[]{:S(2)}) %collective-permute-start.23) | collective-permute-done | bytes 131104 | tf_op jit(solution)/shard_map/ppermute | solution.py:208
  251.4 1.8 fusion.60
  (129 shorter events, 24.4 us)
Async XLA Ops:
  7.6 82.2 %copy-start.5 = (bf16[256,256]{1,0:T(8,128)(2,1)}, bf16[256,256]{1,0:T(8,128)(2,1)S(1)}, u32[]{:S(2)}) copy-start(bf16[256,256]{1,0:T(8,128)(2,1)S(1)} %fusion.35.refs_1_) | copy-start | bytes 393220
  44.2 22.4 %collective-permute-start.1 = (bf16[8,256,256]{2,1,0:T(8,128)(2,1)S(1)}, bf16[8,256,256]{2,1,0:T(8,128)(2,1)S(1)}, u32[]{:S(2)}, u32[]{:S(2)}) collective-permute-start(bf16[8,256,256]{2,1,0:T(8,128)(2,1)S(1)} %all_to_all.25), channel_id=1, source_target_pairs={{0,24},{8,0},{16,8},{24,16},{1,25},{9,1},{17,9},{25,17},{2,26},{10... | collective-permute-start | bytes 3145736 | tf_op jit(solution)/shard_map/ppermute | solution.py:208
  46.6 24.3 %collective-permute-start = (bf16[8,256,256]{2,1,0:T(8,128)(2,1)S(1)}, bf16[8,256,256]{2,1,0:T(8,128)(2,1)S(1)}, u32[]{:S(2)}, u32[]{:S(2)}) collective-permute-start(bf16[8,256,256]{2,1,0:T(8,128)(2,1)S(1)} %all_to_all.25), channel_id=1, source_target_pairs={{0,8},{8,16},{16,24},{24,0},{1,9},{9,17},{17,25},{25,1},{2,10},{10... | collective-permute-start | bytes 3145736 | tf_op jit(solution)/shard_map/ppermute | solution.py:208
  67.5 11.6 %collective-permute-start.3 = (bf16[8,128,256]{2,1,0:T(8,128)(2,1)}, bf16[8,128,256]{2,1,0:T(8,128)(2,1)}, u32[]{:S(2)}, u32[]{:S(2)}) collective-permute-start(bf16[8,128,256]{2,1,0:T(8,128)(2,1)} %slice.238), channel_id=1, source_target_pairs={{0,24},{8,0},{16,8},{24,16},{1,25},{9,1},{17,9},{25,17},{2,26},{10... | collective-permute-start | bytes 1572872 | tf_op jit(solution)/shard_map/ppermute | solution.py:208
  71.8 11.6 %collective-permute-start.2 = (bf16[8,128,256]{2,1,0:T(8,128)(2,1)}, bf16[8,128,256]{2,1,0:T(8,128)(2,1)}, u32[]{:S(2)}, u32[]{:S(2)}) collective-permute-start(bf16[8,128,256]{2,1,0:T(8,128)(2,1)} %slice.237), channel_id=1, source_target_pairs={{0,8},{8,16},{16,24},{24,0},{1,9},{9,17},{17,25},{25,1},{2,10},{10... | collective-permute-start | bytes 1572872 | tf_op jit(solution)/shard_map/ppermute | solution.py:208
  72.4 18.8 %collective-permute-start.4 = (bf16[8,256,256]{2,1,0:T(8,128)(2,1)S(1)}, bf16[8,256,256]{2,1,0:T(8,128)(2,1)}, u32[]{:S(2)}, u32[]{:S(2)}) collective-permute-start(bf16[8,256,256]{2,1,0:T(8,128)(2,1)S(1)} %all_to_all.25), channel_id=1, source_target_pairs={{0,4},{4,0},{1,5},{5,1},{2,6},{6,2},{3,7},{7,3},{8,12},{12,8},{9,1... | collective-permute-start | bytes 3145736 | tf_op jit(solution)/shard_map/ppermute | solution.py:208
  76.1 15.2 %collective-permute-start.6 = (bf16[8,256,256]{2,1,0:T(8,128)(2,1)S(1)}, bf16[8,256,256]{2,1,0:T(8,128)(2,1)}, u32[]{:S(2)}, u32[]{:S(2)}) collective-permute-start(bf16[8,256,256]{2,1,0:T(8,128)(2,1)S(1)} %collective-permute-done.1), channel_id=1, source_target_pairs={{0,4},{4,0},{1,5},{5,1},{2,6},{6,2},{3,7},{7,3},{8,12},{12,8},{9,1... | collective-permute-start | bytes 3145736 | tf_op jit(solution)/shard_map/ppermute | solution.py:208
  76.1 15.2 %collective-permute-start.5 = (bf16[8,256,256]{2,1,0:T(8,128)(2,1)S(1)}, bf16[8,256,256]{2,1,0:T(8,128)(2,1)}, u32[]{:S(2)}, u32[]{:S(2)}) collective-permute-start(bf16[8,256,256]{2,1,0:T(8,128)(2,1)S(1)} %collective-permute-done), channel_id=1, source_target_pairs={{0,4},{4,0},{1,5},{5,1},{2,6},{6,2},{3,7},{7,3},{8,12},{12,8},{9,1... | collective-permute-start | bytes 3145736 | tf_op jit(solution)/shard_map/ppermute | solution.py:208
  79.1 12.2 %collective-permute-start.8 = (bf16[8,128,256]{2,1,0:T(8,128)(2,1)}, bf16[8,128,256]{2,1,0:T(8,128)(2,1)S(1)}, u32[]{:S(2)}, u32[]{:S(2)}) collective-permute-start(bf16[8,128,256]{2,1,0:T(8,128)(2,1)} %collective-permute-done.3.refs_8_), channel_id=1, source_target_pairs={{0,4},{4,0},{1,5},{5,1},{2,6},{6,2},{3,7},{7,3},{8,12},{12,8},{9,1... | collective-permute-start | bytes 1572872 | tf_op jit(solution)/shard_map/ppermute | solution.py:208
  83.4 7.9 %collective-permute-start.7 = (bf16[8,128,256]{2,1,0:T(8,128)(2,1)}, bf16[8,128,256]{2,1,0:T(8,128)(2,1)S(1)}, u32[]{:S(2)}, u32[]{:S(2)}) collective-permute-start(bf16[8,128,256]{2,1,0:T(8,128)(2,1)} %collective-permute-done.2.refs_7_), channel_id=1, source_target_pairs={{0,4},{4,0},{1,5},{5,1},{2,6},{6,2},{3,7},{7,3},{8,12},{12,8},{9,1... | collective-permute-start | bytes 1572872 | tf_op jit(solution)/shard_map/ppermute | solution.py:208
  115.7 65.5 %collective-permute-start.9 = (bf16[4,8,256,256]{3,2,1,0:T(8,128)(2,1)}, bf16[4,8,256,256]{3,2,1,0:T(8,128)(2,1)}, u32[]{:S(2)}, u32[]{:S(2)}) collective-permute-start(bf16[4,8,256,256]{3,2,1,0:T(8,128)(2,1)} %bitcast.114), channel_id=1, source_target_pairs={{0,4},{4,0},{1,5},{5,1},{2,6},{6,2},{3,7},{7,3},{8,12},{12,8},{9,1... | collective-permute-start | bytes 12582920 | tf_op jit(solution)/shard_map/ppermute | solution.py:208
  115.8 8.1 %collective-permute-start.29 = (bf16[6,256,256]{2,1,0:T(8,128)(2,1)}, bf16[6,256,256]{2,1,0:T(8,128)(2,1)S(1)}, u32[]{:S(2)}, u32[]{:S(2)}) collective-permute-start(bf16[6,256,256]{2,1,0:T(8,128)(2,1)} %get-tuple-element.11), channel_id=1, source_target_pairs={{0,4},{4,0},{1,5},{5,1},{2,6},{6,2},{3,7},{7,3},{8,12},{12,8},{9,1... | collective-permute-start | bytes 2359304 | tf_op jit(solution)/shard_map/ppermute | solution.py:208
  174.0 7.1 %collective-permute-start.30 = (bf16[6,256,256]{2,1,0:T(8,128)(2,1)S(1)}, bf16[6,256,256]{2,1,0:T(8,128)(2,1)S(1)}, u32[]{:S(2)}, u32[]{:S(2)}) collective-permute-start(bf16[6,256,256]{2,1,0:T(8,128)(2,1)S(1)} %bitcast.108), channel_id=1, source_target_pairs={{0,4},{4,0},{1,5},{5,1},{2,6},{6,2},{3,7},{7,3},{8,12},{12,8},{9,1... | collective-permute-start | bytes 2359304 | tf_op jit(solution)/shard_map/ppermute | solution.py:208
  182.6 21.2 %collective-permute-start.25 = (bf16[1,128,256]{2,1,0:T(8,128)(2,1)S(1)}, bf16[1,128,256]{2,1,0:T(8,128)(2,1)S(1)}, u32[]{:S(2)}, u32[]{:S(2)}) collective-permute-start(bf16[1,128,256]{2,1,0:T(8,128)(2,1)S(1)} %get-tuple-element.39), channel_id=1, source_target_pairs={{0,8},{8,16},{16,24},{24,0},{1,9},{9,17},{17,25},{25,1},{2,10},{10... | collective-permute-start | bytes 196616 | tf_op jit(solution)/shard_map/ppermute | solution.py:208
  182.9 18.2 %collective-permute-start.27 = (bf16[1,128,256]{2,1,0:T(8,128)(2,1)S(1)}, bf16[1,128,256]{2,1,0:T(8,128)(2,1)S(1)}, u32[]{:S(2)}, u32[]{:S(2)}) collective-permute-start(bf16[1,128,256]{2,1,0:T(8,128)(2,1)S(1)} %get-tuple-element.40), channel_id=1, source_target_pairs={{0,24},{8,0},{16,8},{24,16},{1,25},{9,1},{17,9},{25,17},{2,26},{10... | collective-permute-start | bytes 196616 | tf_op jit(solution)/shard_map/ppermute | solution.py:208
  187.0 18.6 %collective-permute-start.10 = (bf16[3,128,256]{2,1,0:T(8,128)(2,1)S(1)}, bf16[3,128,256]{2,1,0:T(8,128)(2,1)S(1)}, u32[]{:S(2)}, u32[]{:S(2)}) collective-permute-start(bf16[3,128,256]{2,1,0:T(8,128)(2,1)S(1)} %get-tuple-element.37), channel_id=1, source_target_pairs={{0,8},{8,16},{16,24},{24,0},{1,9},{9,17},{17,25},{25,1},{2,10},{10... | collective-permute-start | bytes 589832 | tf_op jit(solution)/shard_map/ppermute | solution.py:208
  187.1 16.9 %collective-permute-start.12 = (bf16[3,128,256]{2,1,0:T(8,128)(2,1)S(1)}, bf16[3,128,256]{2,1,0:T(8,128)(2,1)S(1)}, u32[]{:S(2)}, u32[]{:S(2)}) collective-permute-start(bf16[3,128,256]{2,1,0:T(8,128)(2,1)S(1)} %get-tuple-element.38), channel_id=1, source_target_pairs={{0,24},{8,0},{16,8},{24,16},{1,25},{9,1},{17,9},{25,17},{2,26},{10... | collective-permute-start | bytes 589832 | tf_op jit(solution)/shard_map/ppermute | solution.py:208
  201.0 10.2 %collective-permute-start.17 = (bf16[4,128,256]{2,1,0:T(8,128)(2,1)S(1)}, bf16[4,128,256]{2,1,0:T(8,128)(2,1)S(1)}, u32[]{:S(2)}, u32[]{:S(2)}) collective-permute-start(bf16[4,128,256]{2,1,0:T(8,128)(2,1)S(1)} %get-tuple-element.32), channel_id=1, source_target_pairs={{0,8},{8,16},{16,24},{24,0},{1,9},{9,17},{17,25},{25,1},{2,10},{10... | collective-permute-start | bytes 786440 | tf_op jit(solution)/shard_map/ppermute | solution.py:208
  201.1 6.5 %collective-permute-start.19 = (bf16[4,128,256]{2,1,0:T(8,128)(2,1)S(1)}, bf16[4,128,256]{2,1,0:T(8,128)(2,1)S(1)}, u32[]{:S(2)}, u32[]{:S(2)}) collective-permute-start(bf16[4,128,256]{2,1,0:T(8,128)(2,1)S(1)} %get-tuple-element.33), channel_id=1, source_target_pairs={{0,24},{8,0},{16,8},{24,16},{1,25},{9,1},{17,9},{25,17},{2,26},{10... | collective-permute-start | bytes 786440 | tf_op jit(solution)/shard_map/ppermute | solution.py:208
  203.8 30.9 %collective-permute-start.28 = (bf16[1,256,256]{2,1,0:T(8,128)(2,1)S(1)}, bf16[1,256,256]{2,1,0:T(8,128)(2,1)S(1)}, u32[]{:S(2)}, u32[]{:S(2)}) collective-permute-start(bf16[1,256,256]{2,1,0:T(8,128)(2,1)S(1)} %pad_maximum_fusion.5), channel_id=1, source_target_pairs={{0,24},{8,0},{16,8},{24,16},{1,25},{9,1},{17,9},{25,17},{2,26},{10... | collective-permute-start | bytes 393224 | tf_op jit(solution)/shard_map/ppermute | solution.py:208
  204.0 14.8 %collective-permute-start.13 = (bf16[3,256,256]{2,1,0:T(8,128)(2,1)S(1)}, bf16[3,256,256]{2,1,0:T(8,128)(2,1)S(1)}, u32[]{:S(2)}, u32[]{:S(2)}) collective-permute-start(bf16[3,256,256]{2,1,0:T(8,128)(2,1)S(1)} %pad_maximum_fusion.3), channel_id=1, source_target_pairs={{0,24},{8,0},{16,8},{24,16},{1,25},{9,1},{17,9},{25,17},{2,26},{10... | collective-permute-start | bytes 1179656 | tf_op jit(solution)/shard_map/ppermute | solution.py:208
  205.7 13.1 %collective-permute-start.11 = (bf16[3,256,256]{2,1,0:T(8,128)(2,1)S(1)}, bf16[3,256,256]{2,1,0:T(8,128)(2,1)S(1)}, u32[]{:S(2)}, u32[]{:S(2)}) collective-permute-start(bf16[3,256,256]{2,1,0:T(8,128)(2,1)S(1)} %pad_maximum_fusion.2), channel_id=1, source_target_pairs={{0,8},{8,16},{16,24},{24,0},{1,9},{9,17},{17,25},{25,1},{2,10},{10... | collective-permute-start | bytes 1179656 | tf_op jit(solution)/shard_map/ppermute | solution.py:208
  207.7 22.4 %collective-permute-start.20 = (bf16[4,256,256]{2,1,0:T(8,128)(2,1)S(1)}, bf16[4,256,256]{2,1,0:T(8,128)(2,1)S(1)}, u32[]{:S(2)}, u32[]{:S(2)}) collective-permute-start(bf16[4,256,256]{2,1,0:T(8,128)(2,1)S(1)} %pad_maximum_fusion.1), channel_id=1, source_target_pairs={{0,24},{8,0},{16,8},{24,16},{1,25},{9,1},{17,9},{25,17},{2,26},{10... | collective-permute-start | bytes 1572872 | tf_op jit(solution)/shard_map/ppermute | solution.py:208
  211.3 18.8 %collective-permute-start.18 = (bf16[4,256,256]{2,1,0:T(8,128)(2,1)S(1)}, bf16[4,256,256]{2,1,0:T(8,128)(2,1)S(1)}, u32[]{:S(2)}, u32[]{:S(2)}) collective-permute-start(bf16[4,256,256]{2,1,0:T(8,128)(2,1)S(1)} %pad_maximum_fusion), channel_id=1, source_target_pairs={{0,8},{8,16},{16,24},{24,0},{1,9},{9,17},{17,25},{25,1},{2,10},{10... | collective-permute-start | bytes 1572872 | tf_op jit(solution)/shard_map/ppermute | solution.py:208
  218.8 17.2 %collective-permute-start.26 = (bf16[1,256,256]{2,1,0:T(8,128)(2,1)S(1)}, bf16[1,256,256]{2,1,0:T(8,128)(2,1)S(1)}, u32[]{:S(2)}, u32[]{:S(2)}) collective-permute-start(bf16[1,256,256]{2,1,0:T(8,128)(2,1)S(1)} %pad_maximum_fusion.4), channel_id=1, source_target_pairs={{0,8},{8,16},{16,24},{24,0},{1,9},{9,17},{17,25},{25,1},{2,10},{10... | collective-permute-start | bytes 393224 | tf_op jit(solution)/shard_map/ppermute | solution.py:208
  220.1 18.6 %collective-permute-start.14 = (bf16[256,256]{1,0:T(8,128)(2,1)S(1)}, bf16[256,256]{1,0:T(8,128)(2,1)S(1)}, u32[]{:S(2)}, u32[]{:S(2)}) collective-permute-start(bf16[256,256]{1,0:T(8,128)(2,1)S(1)} %get-tuple-element.34), channel_id=1, source_target_pairs={{0,128},{32,160},{64,192},{96,224},{128,0},{160,32},{192,64},{224,... | collective-permute-start | bytes 393224 | tf_op jit(solution)/shard_map/ppermute | solution.py:208
  230.1 8.6 %collective-permute-start.16 = (bf16[256,256]{1,0:T(8,128)(2,1)S(1)}, bf16[256,256]{1,0:T(8,128)(2,1)S(1)}, u32[]{:S(2)}, u32[]{:S(2)}) collective-permute-start(bf16[256,256]{1,0:T(8,128)(2,1)S(1)} %get-tuple-element.35), channel_id=1, source_target_pairs={{0,160},{32,192},{64,224},{96,0},{128,32},{160,64},{192,96},{224,1... | collective-permute-start | bytes 393224 | tf_op jit(solution)/shard_map/ppermute | solution.py:208
  230.1 11.8 %collective-permute-start.15 = (bf16[256,256]{1,0:T(8,128)(2,1)S(1)}, bf16[256,256]{1,0:T(8,128)(2,1)S(1)}, u32[]{:S(2)}, u32[]{:S(2)}) collective-permute-start(bf16[256,256]{1,0:T(8,128)(2,1)S(1)} %get-tuple-element.36), channel_id=1, source_target_pairs={{0,96},{32,128},{64,160},{96,192},{128,224},{160,0},{192,32},{224,... | collective-permute-start | bytes 393224 | tf_op jit(solution)/shard_map/ppermute | solution.py:208
  234.7 13.2 %collective-permute-start.21 = (bf16[256,256]{1,0:T(8,128)(2,1)S(1)}, bf16[256,256]{1,0:T(8,128)(2,1)S(1)}, u32[]{:S(2)}, u32[]{:S(2)}) collective-permute-start(bf16[256,256]{1,0:T(8,128)(2,1)S(1)} %get-tuple-element.28), channel_id=1, source_target_pairs={{0,64},{32,96},{64,128},{96,160},{128,192},{160,224},{192,0},{224,... | collective-permute-start | bytes 393224 | tf_op jit(solution)/shard_map/ppermute | solution.py:208
  236.0 11.9 %collective-permute-start.24 = (bf16[256,256]{1,0:T(8,128)(2,1)S(1)}, bf16[256,256]{1,0:T(8,128)(2,1)S(1)}, u32[]{:S(2)}, u32[]{:S(2)}) collective-permute-start(bf16[256,256]{1,0:T(8,128)(2,1)S(1)} %get-tuple-element.29), channel_id=1, source_target_pairs={{0,224},{32,0},{64,32},{96,64},{128,96},{160,128},{192,160},{224,1... | collective-permute-start | bytes 393224 | tf_op jit(solution)/shard_map/ppermute | solution.py:208
  238.7 12.7 %collective-permute-start.23 = (bf16[256,256]{1,0:T(8,128)(2,1)S(1)}, bf16[256,256]{1,0:T(8,128)(2,1)S(1)}, u32[]{:S(2)}, u32[]{:S(2)}) collective-permute-start(bf16[256,256]{1,0:T(8,128)(2,1)S(1)} %get-tuple-element.30), channel_id=1, source_target_pairs={{0,32},{32,64},{64,96},{96,128},{128,160},{160,192},{192,224},{224... | collective-permute-start | bytes 393224 | tf_op jit(solution)/shard_map/ppermute | solution.py:208
  238.7 12.7 %collective-permute-start.22 = (bf16[256,256]{1,0:T(8,128)(2,1)S(1)}, bf16[256,256]{1,0:T(8,128)(2,1)S(1)}, u32[]{:S(2)}, u32[]{:S(2)}) collective-permute-start(bf16[256,256]{1,0:T(8,128)(2,1)S(1)} %get-tuple-element.31), channel_id=1, source_target_pairs={{0,192},{32,224},{64,0},{96,32},{128,64},{160,96},{192,128},{224,1... | collective-permute-start | bytes 393224 | tf_op jit(solution)/shard_map/ppermute | solution.py:208
  (13 other events, 177.8 us)
